TPU v7x, 32 devices: a whole 2x2x4 slice. The times are simulated.
32 devices in a mesh: dp: 8 (over z, y), seq: 4 (over x, core).
Axes of the slice: x: 2, y: 2, z: 4, core: 2. Of those that a mesh axis runs over, the one named last changes fastest.
Arguments:
- inputs: bfloat16 [16, 1024, 768], P('dp', 'seq'), may hold values from -6 to 6
- lengths: int32 [16], P('dp'), may hold values from 512 to 1024, as said below
- query_weight: bfloat16 [768, 768], P('dp'), may hold values from -0.3125 to 0.3125
- key_weight: bfloat16 [768, 768], P('dp'), may hold values from -0.3125 to 0.3125
- value_weight: bfloat16 [768, 768], P('dp'), may hold values from -0.21875 to 0.21875
- output_weight: bfloat16 [768, 768], P('dp'), may hold values from -0.625 to 0.625
- up_weight: bfloat16 [768, 3072], P('dp'), may hold values from -0.21875 to 0.21875
- down_weight: bfloat16 [3072, 768], P('dp'), may hold values from -0.15625 to 0.15625
- query_bias: bfloat16 [768], P('dp'), may hold values from -3 to 3
- value_bias: bfloat16 [768], P('dp'), may hold values from -3 to 3
- output_bias: bfloat16 [768], P('dp'), may hold values from -3 to 3
- up_bias: bfloat16 [3072], P('dp'), may hold values from -3 to 3
- down_bias: bfloat16 [768], P('dp'), may hold values from -3 to 3
- first_gain: bfloat16 [768], P('dp'), may hold values from 0.5 to 1.5
- first_shift: bfloat16 [768], P('dp'), may hold values from -2 to 2
- second_gain: bfloat16 [768], P('dp'), may hold values from 0.5 to 1.5
- second_shift: bfloat16 [768], P('dp'), may hold values from -2 to 2
- cotangent: bfloat16 [16, 1024, 768], P('dp', 'seq'), may hold values from -6 to 6
Outputs:
- layer_out: bfloat16 [16, 1024, 768], P('dp', 'seq')
- input_grad: bfloat16 [16, 1024, 768], P('dp', 'seq')
- query_weight_grad: float32 [768, 768], P('dp')
- key_weight_grad: float32 [768, 768], P('dp')
- value_weight_grad: float32 [768, 768], P('dp')
- output_weight_grad: float32 [768, 768], P('dp')
- up_weight_grad: float32 [768, 3072], P('dp')
- down_weight_grad: float32 [3072, 768], P('dp')
- query_bias_grad: float32 [768], P('dp')
- value_bias_grad: float32 [768], P('dp')
- output_bias_grad: float32 [768], P('dp')
- up_bias_grad: float32 [3072], P('dp')
- down_bias_grad: float32 [768], P('dp')
- first_gain_grad: float32 [768], P('dp')
- first_shift_grad: float32 [768], P('dp')
- second_gain_grad: float32 [768], P('dp')
- second_shift_grad: float32 [768], P('dp')
Inputs may be any that keep to these rules, and one draw needn't show every extreme that they name: `lengths`: the number of real tokens of each sequence; its later positions up to 1024 are padding.
All inputs are finite; a program needn't handle non-finite values.
Results may differ from a plain program's by a relative error of at most 0.015.
Values may be sent and summed in bfloat16 or wider, within the bound.
A program may use at most 192 MiB of HBM per device.

v0:
```python
import collections
import functools
import jax
import jax.numpy as jnp
from jax import lax
from jax.experimental import pallas as pl
from jax.experimental.pallas import tpu as pltpu
from jax.sharding import PartitionSpec as P

MESH = pl.DeviceIdType.MESH
HEAD_DIM = 64
eps_norm = 1e-05
masked_score = -1000000000.0


def flip(value, bits):
    bit = 1
    while bit <= bits:
        if bits & bit:
            value = value + bit - 2 * bit * lax.rem(lax.div(value, bit), 2)
        bit *= 2
    return value


class Place:
    def __init__(self, dp_size):
        self.dp = lax.axis_index("dp")
        self.seq = lax.axis_index("seq")
        self.depth = dp_size // 2
        self.z = lax.div(self.dp, 2)
        self.y = lax.rem(self.dp, 2)
        self.core = lax.rem(self.seq, 2)
        self.side = lax.div(self.seq, 2)

    def along_z(self, k):
        return flip(self.dp, 2 * k)

    def peers(self):
        result = [(self.along_z(k), self.seq) for k in range(1, self.depth)]
        result.append((flip(self.dp, 1), self.seq))
        result.append((self.dp, flip(self.seq, 1)))
        result.append((self.dp, flip(self.seq, 2)))
        return result

    def greet(self):
        barrier = pltpu.get_barrier_semaphore()
        peers = self.peers()
        for peer in peers:
            pl.semaphore_signal(barrier, inc=1, device_id=peer, device_id_type=MESH)
        pl.semaphore_wait(barrier, len(peers))


class Gather:
    def __init__(self, place, src, dst, rows, columns, to_columns, split, sems):
        self.place, self.src, self.dst = place, src, dst
        self.columns, self.to_columns, self.split = columns, to_columns, split
        self.first, count = rows
        self.send, self.recv, self.local = sems
        self.depth = place.depth
        self.unit = unit = count // 6
        half = place.core * (3 * unit)
        self.half = (half, 3 * unit)
        self.fetch = (half + place.side * unit, 2 * unit) if split else self.half
        self.far = (half + place.side * (2 * unit), unit)

    def view(self, z, y, window):
        rows = pl.ds(pl.multiple_of(self.first + window[0], self.unit), window[1])
        return self.dst.at[z, y, rows, pl.ds(*self.to_columns)]

    def copy(self, src, dst, index, peer):
        return pltpu.make_async_remote_copy(
            src_ref=src, dst_ref=dst, send_sem=self.send.at[index], recv_sem=self.recv.at[index],
            device_id=peer, device_id_type=MESH,
        )

    def mine(self):
        rows = pl.ds(pl.multiple_of(self.first + self.fetch[0], self.unit), self.fetch[1])
        return self.src.at[rows, pl.ds(*self.columns)]

    def own(self):
        p = self.place
        return pltpu.make_async_copy(self.mine(), self.view(p.z, p.y, self.fetch), self.local)

    def over_z(self, k):
        p = self.place
        return self.copy(self.mine(), self.view(p.z, p.y, self.fetch), k, (p.along_z(k), p.seq))

    def over_y(self):
        p = self.place
        ref = self.view(slice(None), p.y, self.fetch)
        return self.copy(ref, ref, 0, (flip(p.dp, 1), p.seq))

    def over_x(self):
        p, every = self.place, slice(None)
        ref = self.view(every, every, self.far)
        return self.copy(ref, ref, self.depth, (p.dp, flip(p.seq, 2)))

    def across(self):
        p, every = self.place, slice(None)
        ref = self.view(every, every, self.half)
        return self.copy(ref, ref, self.depth + 1, (p.dp, flip(p.seq, 1)))

    def stage_z(self):
        self.own().start()
        for k in range(1, self.depth):
            self.over_z(k).start()

    def stage_y(self):
        self.own().wait()
        for k in range(1, self.depth):
            self.over_z(k).wait_recv()
        self.over_y().start()

    def stage_x(self):
        self.over_y().wait_recv()
        if self.split:
            self.over_x().start()
        else:
            self.across().start()

    def stage_core(self):
        if self.split:
            self.over_x().wait_recv()
            self.across().start()

    def arrive(self):
        self.across().wait_recv()

    def finish(self):
        for k in range(1, self.depth):
            self.over_z(k).wait_send()
        self.over_y().wait_send()
        if self.split:
            self.over_x().wait_send()
        self.across().wait_send()


def gather_sems(dp_size, units):
    n = dp_size // 2 + 2
    return [pltpu.SemaphoreType.DMA((units, n)), pltpu.SemaphoreType.DMA((units, n)), pltpu.SemaphoreType.DMA((units,))]


class Spread:
    def __init__(self, place, src, dst, sems):
        self.place, self.src, self.dst = place, src, dst
        self.send, self.recv, self.local = sems

    def own(self):
        return pltpu.make_async_copy(self.src, self.dst.at[self.place.z, self.place.y], self.local)

    def over_z(self, k):
        p = self.place
        return pltpu.make_async_remote_copy(
            src_ref=self.src, dst_ref=self.dst.at[p.z, p.y], send_sem=self.send.at[k], recv_sem=self.recv.at[k],
            device_id=(p.along_z(k), p.seq), device_id_type=MESH,
        )

    def over_y(self):
        p = self.place
        ref = self.dst.at[:, p.y]
        return pltpu.make_async_remote_copy(
            src_ref=ref, dst_ref=ref, send_sem=self.send.at[0], recv_sem=self.recv.at[0],
            device_id=(flip(p.dp, 1), p.seq), device_id_type=MESH,
        )

    def start(self):
        self.own().start()
        for k in range(1, self.place.depth):
            self.over_z(k).start()

    def forward(self):
        self.own().wait()
        for k in range(1, self.place.depth):
            self.over_z(k).wait_recv()
        self.over_y().start()

    def finish(self):
        for k in range(1, self.place.depth):
            self.over_z(k).wait_send()
        self.over_y().wait()


def gather_steps(units, window):
    count = len(units)
    steps = [[unit.stage_z for unit in units[:window]]]
    for i in range(count + 4):
        step = []
        if i < count:
            step.append(units[i].stage_y)
            if i + window < count:
                step.append(units[i + window].stage_z)
        if 0 <= i - 2 < count:
            step.append(units[i - 2].stage_x)
        if 0 <= i - 4 < count:
            step.append(units[i - 4].stage_core)
        steps.append(step)
    return steps


def weight_units(place, srcs, dsts, plan, sems):
    send, recv, local = sems
    return [
        Gather(place, srcs[s], dsts[d], (first, rows), (column, width), (to, width), split, (send.at[i], recv.at[i], local.at[i]))
        for i, (s, d, first, rows, column, width, to, split) in enumerate(plan)
    ]


class Swap:
    def __init__(self, place, src, dst, send, recv, local):
        side = place.side
        length = src.shape[1]
        own = dst.at[pl.ds(pl.multiple_of(side * length, 8), length)]
        self.here = pltpu.make_async_copy(src.at[side], own, local)
        self.there = pltpu.make_async_remote_copy(
            src_ref=src.at[1 - side], dst_ref=own, send_sem=send, recv_sem=recv,
            device_id=(place.dp, flip(place.seq, 2)), device_id_type=MESH,
        )

    def start(self):
        self.here.start()
        self.there.start()

    def wait(self):
        self.here.wait()
        self.there.wait()


class SwapBack:
    def __init__(self, place, src, dst, send, recv, local):
        side, length = place.side, dst.shape[1]
        block = lambda i: src.at[pl.ds(pl.multiple_of(i * length, length), length)]
        self.here = pltpu.make_async_copy(block(side), dst.at[side], local)
        self.there = pltpu.make_async_remote_copy(
            src_ref=block(1 - side), dst_ref=dst.at[side], send_sem=send, recv_sem=recv,
            device_id=(place.dp, flip(place.seq, 2)), device_id_type=MESH,
        )

    def start(self):
        self.here.start()
        self.there.start()

    def wait(self):
        self.here.wait()
        self.there.wait()


class Reduce:
    def __init__(self, place, src, rows, columns, targets, to_row, split, own, bufs, sems):
        self.place, self.src, self.targets, self.split = place, src, targets, split
        self.columns, self.to_row = columns, to_row
        self.first, count = rows
        self.unit = unit = count // 6
        self.from_core, self.from_x, self.from_y, self.from_z, self.got, self.total = bufs
        self.send, self.recv = sems
        self.depth = place.depth
        self.half = place.core * (3 * unit)
        self.sibling_half = (1 - place.core) * (3 * unit)
        self.keep = (place.side * unit, 2 * unit) if split else (0, 3 * unit)
        self.loads = own is not None
        self.own = own if self.loads else self.view(self.half)

    def view(self, start):
        rows = pl.ds(pl.multiple_of(self.first + start, self.unit), 3 * self.unit)
        return self.src.at[:, :, rows, pl.ds(*self.columns)]

    def rows(self, window):
        return pl.ds(pl.multiple_of(window[0], self.unit), window[1])

    def copy(self, src, dst, index, peer):
        return pltpu.make_async_remote_copy(
            src_ref=src, dst_ref=dst, send_sem=self.send.at[index], recv_sem=self.recv.at[index],
            device_id=peer, device_id_type=MESH,
        )

    def load(self):
        return pltpu.make_async_copy(self.view(self.half), self.own, self.send.at[0])

    def core(self):
        p = self.place
        return self.copy(self.view(self.sibling_half), self.from_core, self.depth, (p.dp, flip(p.seq, 1)))

    def far(self):
        return ((1 - self.place.side) * (2 * self.unit), self.unit)

    def x(self):
        p = self.place
        return self.copy(self.own.at[:, :, self.rows(self.far())], self.from_x, self.depth + 1, (p.dp, flip(p.seq, 2)))

    def y(self):
        p = self.place
        src = self.own.at[:, 1 - p.y, self.rows(self.keep)]
        return self.copy(src, self.from_y.at[:, pl.ds(0, self.keep[1])], self.depth + 2, (flip(p.dp, 1), p.seq))

    def z(self, k):
        p = self.place
        src = self.own.at[flip(p.z, k), p.y, self.rows(self.keep)]
        return self.copy(src, self.from_z.at[k - 1, pl.ds(0, self.keep[1])], k, (p.along_z(k), p.seq))

    def x_last(self):
        p = self.place
        src = self.own.at[p.z, p.y, self.rows(self.keep)]
        return self.copy(src, self.got.at[pl.ds(0, self.keep[1])], self.depth + 3, (p.dp, flip(p.seq, 2)))

    def puts(self):
        p, n = self.place, self.depth
        rows = pl.ds(pl.multiple_of(self.to_row + self.half, self.unit), 3 * self.unit)
        here, there = [], []
        for i, (column, width, out, to) in enumerate(self.targets):
            src, dst = self.total.at[:, pl.ds(column, width)], out.at[rows, pl.ds(to, width)]
            here.append(pltpu.make_async_copy(src, dst, self.send.at[n + 6 + i]))
            there.append(self.copy(src, dst, n + 4 + i, (p.dp, flip(p.seq, 1))))
        return here + there

    def chip(self, z, y, window):
        rows = self.rows(window)
        return self.own[z, y, rows, :].astype(jnp.float32) + self.from_core[z, y, rows, :].astype(jnp.float32)

    def pieces(self, z, y):
        u, side = self.unit, self.place.side
        if not self.split:
            return [((i * u, u), (i * u, u), self.chip(z, y, (i * u, u))) for i in range(3)]
        solo = (side * (2 * u), u)
        gained = self.chip(z, y, solo) + self.from_x[z, y, :, :].astype(jnp.float32)
        return [((u, u), ((1 - side) * u, u), self.chip(z, y, (u, u))), (solo, (side * u, u), gained)]

    def stage_core(self):
        if self.loads:
            self.load().start()
        self.core().start()

    def stage_x(self):
        if self.loads:
            self.load().wait()
        self.core().wait_recv()
        if not self.split:
            return
        rows = self.rows(self.far())

        def body(z, carry):
            for y in range(2):
                self.own[z, y, rows, :] = self.chip(z, y, self.far()).astype(jnp.bfloat16)
            return carry

        lax.fori_loop(0, self.depth, body, 0)
        self.x().start()

    def stage_y(self):
        if self.split:
            self.x().wait_recv()
        y = 1 - self.place.y

        def body(z, carry):
            for at, _, value in self.pieces(z, y):
                self.own[z, y, self.rows(at), :] = value.astype(jnp.bfloat16)
            return carry

        lax.fori_loop(0, self.depth, body, 0)
        self.y().start()

    def column(self, z):
        return [
            (at, kept, value + self.from_y[z, self.rows(kept), :].astype(jnp.float32))
            for at, kept, value in self.pieces(z, self.place.y)
        ]

    def stage_z(self):
        self.y().wait_recv()
        for k in range(1, self.depth):
            z = flip(self.place.z, k)
            for at, _, value in self.column(z):
                self.own[z, self.place.y, self.rows(at), :] = value.astype(jnp.bfloat16)
            self.z(k).start()

    def stage_last(self):
        for k in range(1, self.depth):
            self.z(k).wait_recv()
        p = self.place
        for at, kept, value in self.column(p.z):
            for k in range(1, self.depth):
                value = value + self.from_z[k - 1, self.rows(kept), :].astype(jnp.float32)
            self.own[p.z, p.y, self.rows(at), :] = value.astype(jnp.bfloat16)
        self.x_last().start()

    def stage_out(self):
        self.x_last().wait_recv()
        p, u = self.place, self.unit
        mine = lambda at: self.own[p.z, p.y, self.rows(at), :].astype(jnp.float32)
        got = lambda at: self.got[self.rows(at), :].astype(jnp.float32)
        if self.split:
            side = p.side
            self.total[self.rows((u, u)), :] = mine((u, u)) + got((side * u, u))
            self.total[self.rows((side * (2 * u), u)), :] = mine((side * (2 * u), u))
            self.total[self.rows((2 * u - side * (2 * u), u)), :] = got(((1 - side) * u, u))
        else:
            whole = (0, 3 * u)
            self.total[...] = mine(whole) + got(whole)
        for put in self.puts():
            put.start()

    def finish(self):
        self.core().wait_send()
        if self.split:
            self.x().wait_send()
        self.y().wait_send()
        for k in range(1, self.depth):
            self.z(k).wait_send()
        self.x_last().wait_send()
        for put in self.puts():
            put.wait()


def reduce_scratch(dp_size, units, loads, rows, width):
    z, u = dp_size // 2, rows // 6
    low = lambda count, *shape: pltpu.VMEM((count, *shape, width), jnp.bfloat16)
    return [
        low(loads, z, 2, 3 * u), low(units, z, 2, 3 * u), low(units, z, 2, u), low(units, z, 3 * u), low(units, z - 1, 3 * u),
        low(units, 3 * u), pltpu.VMEM((units, 3 * u, width), jnp.float32),
        pltpu.SemaphoreType.DMA((units, z + 8)), pltpu.SemaphoreType.DMA((units, z + 8)),
    ]


def reduce_units(place, srcs, outs, plan, loads, scratch):
    own, bufs, send, recv = scratch[0], scratch[1:-2], scratch[-2], scratch[-1]
    return [
        Reduce(place, srcs[s], (first, rows), (column, width), [(a, w, outs[o], to) for a, w, o, to in targets], to_row, split,
               own.at[i] if i < loads else None, [b.at[i] for b in bufs], (send.at[i], recv.at[i]))
        for i, (s, first, rows, column, width, to_row, targets, split) in enumerate(plan)
    ]


STAGES = ("stage_core", "stage_x", "stage_y", "stage_z", "stage_last", "stage_out", "finish")


def reduce_steps(units):
    first, steps = -3, collections.defaultdict(list)
    for i, unit in enumerate(units):
        lag = 2 if unit.split else 0
        ages = (-3 if unit.loads else -1, 0, lag, lag + 2, lag + 4, lag + 6, lag + 8)
        for stage, age in zip(STAGES, ages):
            steps[i + age].append((-age, getattr(unit, stage)))
    ticks = range(first, max(steps) + 1)
    return [[call for _, call in sorted(steps[tick], key=lambda pair: pair[0])] for tick in ticks], first


class SumAll:
    def __init__(self, place, src, out, buf, got, send, recv):
        self.place, self.src, self.out, self.buf, self.got, self.send, self.recv = place, src, out, buf, got, send, recv

    def copy(self, stage, slot, peer):
        return pltpu.make_async_remote_copy(
            src_ref=self.buf.at[stage], dst_ref=self.got.at[slot], send_sem=self.send.at[slot], recv_sem=self.recv.at[slot],
            device_id=peer, device_id_type=MESH,
        )

    def copies(self, stage):
        p = self.place
        if stage < 3:
            peer = [(p.dp, flip(p.seq, 1)), (p.dp, flip(p.seq, 2)), (flip(p.dp, 1), p.seq)][stage]
            return [self.copy(stage, stage, peer)]
        return [self.copy(3, 2 + k, (p.along_z(k), p.seq)) for k in range(1, p.depth)]

    def begin(self):
        self.buf[0] = self.src[...]
        for c in self.copies(0):
            c.start()

    def advance(self, stage):
        for c in self.copies(stage):
            c.wait_recv()
        if stage < 3:
            self.buf[stage + 1] = self.buf[stage] + self.got[stage]
            for c in self.copies(stage + 1):
                c.start()
        else:
            z, n = self.place.z, self.place.depth
            pick = lambda i: i
            total = self.buf[3]
            parts = [self.buf[3]] + [self.got[2 + k] for k in range(1, n)]
            total = (parts[0] + parts[1]) + (parts[2] + parts[3])
            self.out[...] = total

    def finish(self):
        for stage in range(4):
            for c in self.copies(stage):
                c.wait_send()


def halves(width):
    lane = lax.broadcasted_iota(jnp.int32, (1, width), 1)
    return lane


def key_extra(extra_ref, length, core, rows, first_pos):
    block = rows // 4
    row = lax.broadcasted_iota(jnp.int32, (rows, 128), 0)
    lane = lax.broadcasted_iota(jnp.int32, (rows, 128), 1)
    part = row // block
    owner = jnp.where(part < 2, core, 1 - core)
    position = row - part * block + (owner + 2 * lax.rem(part, 2)) * block
    dead = jnp.where(position < length, 0.0, masked_score)
    for parity in range(2):
        base = HEAD_DIM * (1 - parity)
        at = lane - base
        value = jnp.where(at == 0, dead, jnp.where((at > 0) & (at < 4), -1.0, 0.0))
        extra_ref[parity, :, :] = value.astype(jnp.bfloat16)


def split3(value):
    high = value.astype(jnp.bfloat16).astype(jnp.float32)
    rest = value - high
    mid = rest.astype(jnp.bfloat16).astype(jnp.float32)
    return high, mid, rest - mid


def nt(a, b):
    return lax.dot_general(a, b, (((1,), (1,)), ((), ())), preferred_element_type=jnp.float32)


def nn(a, b):
    return jnp.dot(a, b, preferred_element_type=jnp.float32)


def greet_sibling(peer):
    barrier = pltpu.get_barrier_semaphore()
    pl.semaphore_signal(barrier, inc=1, device_id=peer, device_id_type=MESH)
    pl.semaphore_wait(barrier, 1)


def forward_slab(j, tile, qkv_ref, other_ref, extra_ref, ctx_ref, lse_ref, between=None):
    rows, width = ctx_ref.shape
    lane = lax.broadcasted_iota(jnp.int32, (1, 128), 1)
    cols = lambda base: pl.ds(base + 128 * j if isinstance(j, int) else pl.multiple_of(base + 128 * j, 128), 128)
    keys = jnp.concatenate([qkv_ref[:, cols(width)], other_ref[:, cols(0)]], axis=0)
    values = jnp.concatenate([qkv_ref[:, cols(2 * width)], other_ref[:, cols(width)]], axis=0)
    queries = qkv_ref[:, cols(0)]
    outs, stats = [], []
    for parity in range(2):
        mine = (lane < HEAD_DIM) if parity == 0 else (lane >= HEAD_DIM)
        mark = jnp.where(lane == HEAD_DIM * (1 - parity), 1.0, 0.0).astype(jnp.bfloat16)
        k_h = jnp.where(mine, keys, extra_ref[parity])
        v_h = jnp.where(mine, values, jnp.ones_like(values))
        q_h = jnp.where(mine, queries * jnp.bfloat16(HEAD_DIM ** -0.5), mark)
        pieces, tops = [], []
        for t in range(rows // tile):
            scores = nt(q_h[t * tile:(t + 1) * tile], k_h)
            top = jnp.max(scores, axis=-1, keepdims=True)
            pieces.append(nn(jnp.exp(scores - top).astype(jnp.bfloat16), v_h))
            tops.append(top)
        out, top = jnp.concatenate(pieces, axis=0), jnp.concatenate(tops, axis=0)
        other = HEAD_DIM * (1 - parity)
        total = out[:, other:other + 1]
        outs.append(out / total)
        stats.append(top + jnp.log(total))
        if between is not None:
            between()
    ctx_ref[:, cols(0)] = jnp.where(lane < HEAD_DIM, outs[0], outs[1]).astype(jnp.bfloat16)
    lse_ref[...] = jnp.where(lane == 2 * j, stats[0], jnp.where(lane == 2 * j + 1, stats[1], lse_ref[...]))


def backward_slab(j, block, ins, work, dk_ref, dv_ref, out_ref, between=None):
    qkv_ref, other_ref, ctx_ref, grad_ref, lse_ref = ins
    extra_ref, k_ref, v_ref, q_ref, g_ref, kt_ref, dq_ref = work
    rows, width = ctx_ref.shape
    low = jnp.bfloat16
    lane = lax.broadcasted_iota(jnp.int32, (1, 128), 1)
    sub = lax.broadcasted_iota(jnp.int32, (128, 1), 0)
    cols = lambda base: pl.ds(base + 128 * j if isinstance(j, int) else pl.multiple_of(base + 128 * j, 128), 128)
    keys = jnp.concatenate([qkv_ref[:, cols(width)], other_ref[:, cols(0)]], axis=0)
    values = jnp.concatenate([qkv_ref[:, cols(2 * width)], other_ref[:, cols(width)]], axis=0)
    queries = qkv_ref[:, cols(0)] * jnp.bfloat16(HEAD_DIM ** -0.5)
    grads = grad_ref[:, cols(0)]
    along = grads.astype(jnp.float32) * ctx_ref[:, cols(0)].astype(jnp.float32)
    lse = lse_ref[...]
    for parity in range(2):
        mine = (lane < HEAD_DIM) if parity == 0 else (lane >= HEAD_DIM)
        at = lane - HEAD_DIM * (1 - parity)
        delta = jnp.sum(jnp.where(mine, along, 0.0), axis=-1, keepdims=True)
        stat = jnp.sum(jnp.where(lane == 2 * j + parity, lse, 0.0), axis=-1, keepdims=True)
        s0, s1, s2 = split3(stat)
        d0, d1, d2 = split3(delta)
        q_more = jnp.where(at == 0, 1.0, jnp.where(at == 1, s0, jnp.where(at == 2, s1, jnp.where(at == 3, s2, 0.0)))).astype(low)
        g_more = jnp.where(at == 1, d0, jnp.where(at == 2, d1, jnp.where(at == 3, d2, 0.0))).astype(low)
        k_ref[parity] = jnp.where(mine, keys, extra_ref[parity])
        v_ref[parity] = jnp.where(mine, values, extra_ref[parity])
        q_ref[parity] = jnp.where(mine, queries, q_more)
        g_ref[parity] = jnp.where(mine, grads, g_more)
        kt_ref[parity] = jnp.where((sub < HEAD_DIM) if parity == 0 else (sub >= HEAD_DIM), keys.T, jnp.zeros((128, 2 * rows), low))
    dq_ref[...] = jnp.zeros_like(dq_ref)

    def part(b, carry):
        span = pl.ds(pl.multiple_of(b * block, block), block)
        made = []
        for parity in range(2):
            q_h, g_h = q_ref[parity], g_ref[parity]
            prob = jnp.exp(nt(k_ref[parity, span, :], q_h))
            slope = nt(v_ref[parity, span, :], g_h)
            ds = (prob * slope).astype(low)
            dv = nn(prob.astype(low), g_h)
            dk = nn(ds, q_h)
            dq_ref[...] += nn(kt_ref[parity, :, span], ds)
            made.append((dk, dv))
        dk_ref[span, :] = jnp.where(lane < HEAD_DIM, made[0][0], made[1][0])
        dv_ref[span, :] = jnp.where(lane < HEAD_DIM, made[0][1], made[1][1])
        return carry

    count, cuts = 2 * rows // block, (0, 2, 4) if between is not None else (0, 4)
    for low_cut, high_cut in zip(cuts, cuts[1:]):
        if low_cut:
            between()
        lax.fori_loop(low_cut * count // 4, high_cut * count // 4, part, 0)
    out_ref[:, cols(0)] = (dq_ref[...].T * (HEAD_DIM ** -0.5)).astype(low)


def backward_work(rows):
    low = lambda *shape: pltpu.VMEM(shape, jnp.bfloat16)
    return [
        low(2, 2 * rows, 128), low(2, 2 * rows, 128), low(2, 2 * rows, 128), low(2, rows, 128), low(2, rows, 128),
        low(2, 128, 2 * rows), pltpu.VMEM((128, rows), jnp.float32),
    ]


class Give:
    def __init__(self, peer, dk_ref, dv_ref, got_ref, out_ref, rows, width, sems):
        self.peer, self.pair, self.got_ref, self.out_ref = peer, (dk_ref, dv_ref), got_ref, out_ref
        self.rows, self.width, (self.send, self.recv) = rows, width, sems

    def copy(self, j, which):
        return pltpu.make_async_remote_copy(
            src_ref=self.pair[which].at[lax.rem(j, 2), pl.ds(self.rows, self.rows)], dst_ref=self.got_ref.at[j, which],
            send_sem=self.send.at[j, which], recv_sem=self.recv.at[j, which], device_id=self.peer, device_id_type=MESH,
        )

    def start(self, j):
        for which in range(2):
            self.copy(j, which).start()

    def take(self, j):
        for which in range(2):
            self.copy(j, which).wait()
            total = self.pair[which][lax.rem(j, 2), pl.ds(0, self.rows), :] + self.got_ref[j, which]
            start = (1 + which) * self.width + j * 128
            self.out_ref[:, pl.ds(start if isinstance(j, int) else pl.multiple_of(start, 128), 128)] = total.astype(jnp.bfloat16)


def forward_kernel(tile, length_ref, qkv_ref, ctx_ref, lse_ref, other_ref, extra_ref, send, recv):
    seq = lax.axis_index("seq")
    core, side = lax.rem(seq, 2), lax.div(seq, 2)
    peer = (lax.axis_index("dp"), flip(seq, 1))
    rows, width = ctx_ref.shape
    greet_sibling(peer)
    swap = pltpu.make_async_remote_copy(
        src_ref=qkv_ref.at[:, pl.ds(width, 2 * width)], dst_ref=other_ref, send_sem=send, recv_sem=recv,
        device_id=peer, device_id_type=MESH,
    )
    swap.start()
    key_extra(extra_ref, jnp.where(side == 0, length_ref[0], length_ref[1]), core, 2 * rows, 0)
    swap.wait()
    lse_ref[...] = jnp.zeros_like(lse_ref)

    def slab(j, carry):
        forward_slab(j, tile, qkv_ref, other_ref, extra_ref, ctx_ref, lse_ref)
        return carry

    lax.fori_loop(0, width // 128, slab, 0)


def attend_forward(lengths, qkv):
    rows, width = qkv.shape[0], qkv.shape[1] // 3
    vmem = pl.BlockSpec(memory_space=pltpu.VMEM)
    return pl.pallas_call(
        functools.partial(forward_kernel, min(256, rows)),
        out_shape=[
            jax.ShapeDtypeStruct((rows, width), jnp.bfloat16),
            jax.ShapeDtypeStruct((rows, 128), jnp.float32),
            jax.ShapeDtypeStruct((rows, 2 * width), jnp.bfloat16),
        ],
        in_specs=[pl.BlockSpec(memory_space=pltpu.SMEM), vmem],
        out_specs=[vmem] * 3,
        scratch_shapes=[pltpu.VMEM((2, 2 * rows, 128), jnp.bfloat16), pltpu.SemaphoreType.DMA, pltpu.SemaphoreType.DMA],
        compiler_params=pltpu.CompilerParams(collective_id=1, has_side_effects=True, vmem_limit_bytes=48 << 20),
        name="attend_forward",
    )(lengths, qkv)


def backward_kernel(block, length_ref, *refs):
    ins, out_ref, work, (dk_ref, dv_ref, got_ref, send, recv) = refs[:5], refs[5], refs[6:13], refs[13:]
    seq = lax.axis_index("seq")
    core, side = lax.rem(seq, 2), lax.div(seq, 2)
    peer = (lax.axis_index("dp"), flip(seq, 1))
    rows, width = ins[2].shape
    greet_sibling(peer)
    key_extra(work[0], jnp.where(side == 0, length_ref[0], length_ref[1]), core, 2 * rows, 0)
    give = Give(peer, dk_ref, dv_ref, got_ref, out_ref, rows, width, (send, recv))
    for j in range(width // 128):
        if j >= 2:
            give.take(j - 2)
        backward_slab(j, block, ins, work, dk_ref.at[j % 2], dv_ref.at[j % 2], out_ref)
        give.start(j)
    for j in range(width // 128 - 2, width // 128):
        give.take(j)


def attend_backward(lengths, qkv, other, ctx, grad, lse):
    rows, width = ctx.shape
    slabs = width // 128
    vmem = pl.BlockSpec(memory_space=pltpu.VMEM)
    return pl.pallas_call(
        functools.partial(backward_kernel, min(256, rows)),
        out_shape=jax.ShapeDtypeStruct(qkv.shape, jnp.bfloat16),
        in_specs=[pl.BlockSpec(memory_space=pltpu.SMEM)] + [vmem] * 5,
        out_specs=vmem,
        scratch_shapes=backward_work(rows) + give_scratch(rows, slabs),
        compiler_params=pltpu.CompilerParams(collective_id=2, has_side_effects=True, vmem_limit_bytes=56 << 20),
        name="attend_backward",
    )(lengths, qkv, other, ctx, grad, lse)


def give_scratch(rows, slabs):
    full = lambda *shape: pltpu.VMEM(shape, jnp.float32)
    return [
        full(2, 2 * rows, 128), full(2, 2 * rows, 128), full(slabs, 2, rows, 128),
        pltpu.SemaphoreType.DMA((slabs, 2)), pltpu.SemaphoreType.DMA((slabs, 2)),
    ]


def encode_kernel(dp_size, plan, window, tile, length_ref, *refs):
    srcs, vec, rows_in, cot_in = refs[:6], refs[6], refs[7], refs[8]
    results = refs[9:27]
    (send, recv, local, vec_buf, vec_send, vec_recv, vec_local, swap_sem, *bufs, x_buf, qkv_ref, ctx_ref, lse_ref, other_ref,
     norm_ref, unit_ref, scale_ref, act_ref, slope_ref, grad_ref, layer_ref, sums_ref, cot_buf, flat_vec, bias_up, sum_ref, out_sem,
     extra_ref, kv_send, kv_recv) = refs[27:]
    w_buf = bufs[0]
    place = Place(dp_size)
    rows, width = ctx_ref.shape
    place.greet()
    moves = [Swap(place, a, b, swap_sem.at[i, 0], swap_sem.at[i, 1], swap_sem.at[i, 2])
             for i, (a, b) in enumerate(((rows_in, x_buf), (cot_in, cot_buf)))]
    spread = Spread(place, vec, vec_buf, (vec_send, vec_recv, vec_local))
    units = weight_units(place, srcs, bufs, plan, (send, recv, local))
    steps = gather_steps(units, window)
    kept = (*bufs, x_buf, qkv_ref, ctx_ref, lse_ref, other_ref, norm_ref, unit_ref, scale_ref, act_ref, slope_ref, grad_ref,
            layer_ref, sums_ref, flat_vec)
    puts = [pltpu.make_async_copy(a, b, out_sem.at[i]) for i, (a, b) in enumerate(zip(kept, results))]
    clock = iter(steps)

    def run(count=1):
        for _ in range(count):
            for call in next(clock, ()):
                call()

    spread.start()
    moves[0].start()
    run()
    spread.forward()
    run()
    key_extra(extra_ref, jnp.where(place.side == 0, length_ref[0], length_ref[1]), place.core, 2 * rows, 0)
    lse_ref[...] = jnp.zeros_like(lse_ref)
    run()
    spread.finish()
    lane = lax.broadcasted_iota(jnp.int32, (8, 128), 1)
    total = jnp.zeros((8, width), jnp.float32)
    share = width // dp_size
    for owner in range(dp_size):
        piece = jnp.where(lane < share, vec_buf[owner // 2, owner % 2, 0:8, :], 0.0)
        padded = jnp.concatenate([piece, jnp.zeros((8, width - 128), jnp.float32)], axis=1)
        total = total + (pltpu.roll(padded, owner * share, 1) if owner else padded)
    flat_vec[...] = total
    wide = bias_up.shape[1] // dp_size // 128
    for owner in range(dp_size):
        for i in range(wide):
            bias_up[:, pl.ds((owner * wide + i) * 128, 128)] = vec_buf[owner // 2, owner % 2, 8 + i:9 + i, :]
    run(9)
    moves[0].wait()
    puts[4].start()

    def fetch(first):
        for i in range(first, first + 2):
            units[i].arrive()

    step = 256

    def project(first, count):
        def body(t, carry):
            cols = pl.ds(pl.multiple_of(first + t * step, step), step)
            weight = w_buf[:, :, :, cols].reshape(width, step)
            qkv_ref[:, cols] = nn(x_buf[...], weight).astype(jnp.bfloat16)
            return carry

        lax.fori_loop(0, count, body, 0)

    def project_bias(first, row):
        def body(t, carry):
            cols = pl.ds(pl.multiple_of(first + t * step, step), step)
            bias = flat_vec[row:row + 1, pl.ds(pl.multiple_of(t * step, step), step)]
            weight = w_buf[:, :, :, cols].reshape(width, step)
            qkv_ref[:, cols] = (nn(x_buf[...], weight) + bias).astype(jnp.bfloat16)
            return carry

        lax.fori_loop(0, width // step, body, 0)

    fetch(0)
    project(width, width // step)
    run()
    fetch(2)
    project_bias(2 * width, 1)
    swap = pltpu.make_async_remote_copy(
        src_ref=qkv_ref.at[:, pl.ds(width, 2 * width)], dst_ref=other_ref, send_sem=kv_send, recv_sem=kv_recv,
        device_id=(place.dp, flip(place.seq, 1)), device_id_type=MESH,
    )
    swap.start()
    run()
    fetch(4)
    project_bias(0, 0)
    run()
    swap.wait()
    counts = []
    taken = [step for step in clock]
    clock = iter(taken)

    def forward_two(j, carry):
        def between():
            counts.append(len(counts))
            for k in range(width // 128):
                index = 2 * k + len(counts) - 1
                if index < len(taken):
                    @pl.when(j == k)
                    def _():
                        for call in taken[index]:
                            call()

        forward_slab(j, tile, qkv_ref, other_ref, extra_ref, ctx_ref, lse_ref, between)

        @pl.when(j == 1)
        def _():
            moves[1].start()

        return carry

    lax.fori_loop(0, width // 128, forward_two, 0)
    for _ in range(2 * (width // 128)):
        next(clock, ())
    for i in (0, 5, 6, 7, 8):
        puts[i].start()
    low = jnp.bfloat16
    vec_row = lambda i, cols=slice(None): flat_vec[i:i + 1, cols]

    def out_part(t, carry):
        cols = pl.ds(pl.multiple_of(t * step, step), step)
        weight = bufs[1][:, :, :, cols].reshape(width, step)
        sum_ref[:, cols] = x_buf[:, cols].astype(jnp.float32) + (nn(ctx_ref[...], weight) + vec_row(2, cols))
        return carry

    units[6].arrive()
    units[7].arrive()
    lax.fori_loop(0, width // step, out_part, 0)
    puts[1].start()
    run()
    chunk = 128

    def stats(value):
        centred = value - jnp.mean(value, axis=-1, keepdims=True)
        scale = lax.rsqrt(jnp.mean(centred * centred, axis=-1, keepdims=True) + eps_norm)
        return centred * scale, scale

    def first_rows(t, carry):
        at = pl.ds(pl.multiple_of(t * chunk, chunk), chunk)
        unit, scale = stats(sum_ref[at, :])
        unit_ref[at, :] = unit
        scale_ref[at, :] = jnp.broadcast_to(scale, (chunk, 128))
        norm_ref[at, :] = (unit * vec_row(4) + vec_row(5)).astype(low)
        return carry

    lax.fori_loop(0, rows // chunk, first_rows, 0)
    for i in (9, 10, 11):
        puts[i].start()
    run()
    hidden = act_ref.shape[1]

    def up_part(t, carry):
        cols = pl.ds(pl.multiple_of(t * step, step), step)
        weight = bufs[2][:, :, :, cols].reshape(width, step)
        value = nn(norm_ref[...], weight) + bias_up[:, cols]
        below = 0.5 + 0.5 * lax.erf(value * (0.5 ** 0.5))
        act_ref[:, cols] = (value * below).astype(low)
        slope_ref[:, cols] = (below + value * jnp.exp(-0.5 * value * value) * 0.3989422804014327).astype(low)
        return carry

    for j in range(hidden // width):
        for unit in units[8 + 2 * j:10 + 2 * j]:
            unit.arrive()
        ahead = [next(clock, ()) for _ in range(width // step)]
        base = j * width // step

        def up_step(t, carry):
            up_part(t, carry)
            for k, calls in enumerate(ahead):
                if calls:
                    @pl.when(t == base + k)
                    def _():
                        for call in calls:
                            call()
            return carry

        lax.fori_loop(base, base + width // step, up_step, 0)
    for i in (2, 12, 13):
        puts[i].start()
    run(len(steps))
    half = width // 2
    count = hidden // width
    for h in range(2):
        for unit in units[-2 * count + h * count:len(units) - count + h * count]:
            unit.arrive()
        cols = pl.ds(h * half, half)
        weight = bufs[3][:, :, :, cols].reshape(hidden, half)
        sum_ref[:, cols] = norm_ref[:, cols].astype(jnp.float32) + (nn(act_ref[...], weight) + vec_row(3, cols))
    puts[3].start()
    moves[1].wait()
    length = jnp.where(place.side == 0, length_ref[0], length_ref[1])
    block = rows // 2
    sums_ref[...] = jnp.zeros_like(sums_ref)

    def second_rows(t, carry):
        at = pl.ds(pl.multiple_of(t * chunk, chunk), chunk)
        unit, scale = stats(sum_ref[at, :])
        layer_ref[at, :] = (unit * vec_row(6) + vec_row(7)).astype(low)
        row = lax.broadcasted_iota(jnp.int32, (chunk, 1), 0) + t * chunk
        position = lax.rem(row, block) + (place.core + 2 * lax.div(row, block)) * block
        given = jnp.where(position < length, cot_buf[at, :].astype(jnp.float32), 0.0)
        e = given * vec_row(6)
        first = jnp.mean(e, axis=-1, keepdims=True)
        second = jnp.mean(e * unit, axis=-1, keepdims=True)
        grad = scale * (e - first - unit * second)
        grad_ref[at, :] = grad
        for i, value in enumerate((given * unit, given, grad.astype(low).astype(jnp.float32))):
            sums_ref[i:i + 1, :] += jnp.sum(value, axis=0, keepdims=True)
        return carry

    lax.fori_loop(0, rows // chunk, second_rows, 0)
    for i in (14, 15, 16, 17):
        puts[i].start()
    for unit in units:
        unit.finish()
    for put in puts:
        put.wait()


def encode(dp_size, lengths, weights, dst_shapes, plan, vec, rows_in, cotangent, window=3):
    groups, length, width = rows_in.shape
    rows, z, slots = groups * length, dp_size // 2, dp_size // 2
    anywhere = pl.BlockSpec(memory_space=pl.ANY)
    low = lambda *shape: jax.ShapeDtypeStruct(shape, jnp.bfloat16)
    full = lambda *shape: jax.ShapeDtypeStruct(shape, jnp.float32)
    dma = pltpu.SemaphoreType.DMA
    hidden = dst_shapes[2][1]
    kept = [low(z, 2, *shape) for shape in dst_shapes] + [
        low(rows, width), low(rows, 3 * width), low(rows, width), full(rows, 128), low(rows, 2 * width),
        low(rows, width), full(rows, width), full(rows, 128), low(rows, hidden), low(rows, hidden), full(rows, width),
        low(rows, width), full(8, width), full(8, width),
    ]
    hold = lambda a: pltpu.VMEM(a.shape, a.dtype)
    return pl.pallas_call(
        functools.partial(encode_kernel, dp_size, plan, window, min(256, rows)),
        out_shape=kept,
        in_specs=[pl.BlockSpec(memory_space=pltpu.SMEM)] + [anywhere] * 9,
        out_specs=[anywhere] * len(kept),
        scratch_shapes=gather_sems(dp_size, len(plan)) + [
            pltpu.VMEM((z, 2, *vec.shape), jnp.float32), dma((slots,)), dma((slots,)), dma, dma((2, 3)),
            *[hold(a) for a in kept[:-1]], pltpu.VMEM((rows, width), jnp.bfloat16), hold(kept[-1]),
            pltpu.VMEM((1, hidden), jnp.float32), pltpu.VMEM((rows, width), jnp.float32), dma((len(kept),)),
            pltpu.VMEM((2, 2 * rows, 128), jnp.bfloat16), dma, dma,
        ],
        compiler_params=pltpu.CompilerParams(collective_id=0, has_side_effects=True, vmem_limit_bytes=60 << 20),
        name="encode",
    )(lengths, *weights, vec, rows_in, cotangent)


class Stream:
    def __init__(self, pieces, buf, sem):
        self.copies = [pltpu.make_async_copy(piece, buf.at[i % 2], sem.at[i % 2]) for i, piece in enumerate(pieces)]
        self.buf = buf
        for copy in self.copies[:2]:
            copy.start()

    def get(self, i):
        self.copies[i].wait()
        return self.buf.at[i % 2]

    def next(self, i):
        if i + 2 < len(self.copies):
            self.copies[i + 2].start()


class Stage:
    def __init__(self, buf, sem):
        self.buf, self.sem, self.flying = buf, sem, []

    def put(self, value, dst):
        slot = len(self.flying) % 2
        if len(self.flying) >= 2:
            self.flying[-2].wait()
        self.buf[slot] = value
        self.flying.append(pltpu.make_async_copy(self.buf.at[slot], dst, self.sem.at[slot]))
        self.flying[-1].start()

    def drain(self):
        for copy in self.flying[-2:]:
            copy.wait()
        self.flying = []


def column_sum(value):
    return jnp.sum(value.astype(jnp.float32), axis=0, keepdims=True)


def decode_kernel(dp_size, plan, loads, block, length_ref, *refs):
    (qkv_in, other_in, ctx_in, lse_in, x_in, qkv_w, out_w, up_w, down_w, norm_in, unit_in, scale_in, act_in, slope_in,
     grad_in, layer_in, sums_in, vec_in) = refs[:18]
    outs, vec_outs, layer_out, input_out, parts = refs[18:24], refs[24:33], refs[33], refs[34], refs[35:38]
    scratch = refs[38:]
    got_ref, give_send, give_recv, rows_ref, layer_ref, base_ref, ctx_ref, lse_ref, cgrad_ref, sums_ref, vec_ref = scratch[:11]
    small_ref, small_out, swap_sem, load_sem, late_sem, stream_sem, grad_ref = scratch[11:18]
    small_scratch, reduce_refs = scratch[18:22], scratch[22:]
    place = Place(dp_size)
    rows, width = ctx_ref.shape
    hidden = act_in.shape[1]
    slabs, low, step = width // 128, jnp.bfloat16, 256
    half = width // 2
    early = [pltpu.make_async_copy(a, b, load_sem.at[i]) for i, (a, b) in enumerate((
        (grad_in, base_ref), (layer_in, layer_ref), (ctx_in, ctx_ref), (lse_in, lse_ref), (sums_in, sums_ref), (vec_in, vec_ref)))]
    for copy in early:
        copy.start()
    place.greet()
    moves = [SwapBack(place, a, b, swap_sem.at[i, 0], swap_sem.at[i, 1], swap_sem.at[i, 2])
             for i, (a, b) in enumerate(((layer_ref, layer_out), (rows_ref, input_out)))]
    units = reduce_units(place, (*parts, grad_ref), outs, plan, loads, reduce_refs)
    small = SumAll(place, small_ref, small_out, *small_scratch)
    steps, first = reduce_steps(units)
    clock = iter(range(first, first + len(steps)))

    def tick(count=1):
        for _ in range(count):
            for call in steps[next(clock) - first]:
                call()

    def feed_backward(act_buf, slope_buf, down_buf, up_buf, low_ref, up_low, norm_ref, norm_t, unit_ref, scale_ref, out_buf, ctx_t,
                      tall, flat):
        chunks = hidden // width
        cut = lambda ref, i: ref.at[:, pl.ds(i * width, width)]
        acts = Stream([cut(act_in, i) for i in range(chunks)], act_buf, stream_sem.at[0])
        slopes = Stream([cut(slope_in, i) for i in range(chunks)], slope_buf, stream_sem.at[1])
        downs = Stream([down_w.at[pl.ds(i * width, width)] for i in range(chunks)], down_buf, stream_sem.at[2])
        ups = Stream([cut(up_w, i) for i in range(chunks)], up_buf, stream_sem.at[3])
        others = [pltpu.make_async_copy(a, b, late_sem.at[i]) for i, (a, b) in enumerate((
            (norm_in, norm_ref), (unit_in, unit_ref), (scale_in, scale_ref), (out_w, out_buf)))]
        for copy in others:
            copy.start()
        for copy in early:
            copy.wait()
        moves[0].start()
        small_ref[...] = jnp.zeros_like(small_ref)
        small_ref[3:4, :] = sums_ref[2:3, :]
        small_ref[6:8, :] = sums_ref[0:2, :]
        low_ref[...] = base_ref[...].astype(low)
        stage = Stage(tall, stream_sem.at[4])
        each = hidden // dp_size
        for i in range(chunks):
            act = acts.get(i)
            for o in range(width // each):
                owner = i * (width // each) + o
                value = nn(act[:, o * each:(o + 1) * each].T, low_ref[...])
                stage.put(value.astype(low), parts[0].at[owner // 2, owner % 2])
            acts.next(i)
        stage.drain()
        tick(-first)
        others[0].wait()
        norm_t[...] = norm_ref[...].T
        stage = Stage(flat, stream_sem.at[4])
        shape = (place.depth, 2, width // dp_size, half)
        for i in range(chunks):
            slope, down = slopes.get(i), downs.get(i)

            def slope_part(t, carry):
                cols = pl.ds(pl.multiple_of(t * step, step), step)
                value = nt(low_ref[...], down[cols, :]) * slope[:, cols].astype(jnp.float32)
                up_low[:, cols] = value.astype(low)
                return carry

            lax.fori_loop(0, width // step, slope_part, 0)
            slopes.next(i)
            downs.next(i)
            small_ref[8 + i:9 + i, :] = column_sum(up_low[...])
            for h in range(2):
                value = nn(norm_t[...], up_low[:, h * half:(h + 1) * half]).astype(low)
                stage.put(value.reshape(shape), parts[1].at[:, :, :, pl.ds(i * width + h * half, half)])
            tick()
            up = ups.get(i)

            def back_part(t, carry):
                cols = pl.ds(pl.multiple_of(t * step, step), step)
                base_ref[:, cols] += nt(up_low[...], up[cols, :])
                return carry

            lax.fori_loop(0, width // step, back_part, 0)
            ups.next(i)
            stage.drain()
            tick()
        for copy in others[1:]:
            copy.wait()
        chunk = 128
        gain = vec_ref[4:5, :]

        def first_rows(t, carry):
            at = pl.ds(pl.multiple_of(t * chunk, chunk), chunk)
            given, unit = base_ref[at, :], unit_ref[at, :]
            e = given * gain
            mean = jnp.mean(e, axis=-1, keepdims=True)
            along = jnp.mean(e * unit, axis=-1, keepdims=True)
            grad = scale_ref[at, :][:, :1] * (e - mean - unit * along)
            base_ref[at, :] = grad
            low_ref[at, :] = grad.astype(low)
            for i, value in ((4, given * unit), (5, given), (2, grad.astype(low))):
                small_ref[i:i + 1, :] += column_sum(value)
            return carry

        lax.fori_loop(0, rows // chunk, first_rows, 0)
        ctx_t[...] = ctx_ref[...].T
        for h in range(2):
            value = nn(ctx_t[...], low_ref[:, h * half:(h + 1) * half]).astype(low)
            stage.put(value.reshape(shape), parts[2].at[:, :, :, pl.ds(h * half, half)])
        tick()

        def context_part(t, carry):
            cols = pl.ds(pl.multiple_of(t * step, step), step)
            cgrad_ref[:, cols] = nt(low_ref[...], out_buf[cols, :]).astype(low)
            return carry

        lax.fori_loop(0, width // step, context_part, 0)
        stage.drain()
        tick()

    lows = lambda *shape: pltpu.VMEM(shape, low)
    full = lambda *shape: pltpu.VMEM(shape, jnp.float32)
    pl.run_scoped(
        feed_backward, lows(2, rows, width), lows(2, rows, width), lows(2, width, width), lows(2, width, width), lows(rows, width),
        lows(rows, width), lows(rows, width), lows(width, rows), full(rows, width), full(rows, 128), lows(width, width),
        lows(width, rows), lows(2, hidden // dp_size, width), lows(2, place.depth, 2, width // dp_size, half),
    )

    def attend(qkv_ref, other_ref, x_ref, xt_ref, w_ref, d_ref, dk_ref, dv_ref, *work):
        late = [pltpu.make_async_copy(a, b, late_sem.at[i]) for i, (a, b) in enumerate((
            (qkv_in, qkv_ref), (other_in, other_ref), (x_in, x_ref), (qkv_w, w_ref)))]
        for copy in late:
            copy.start()
        ins = (qkv_ref, other_ref, ctx_ref, cgrad_ref, lse_ref)
        give = Give((place.dp, flip(place.seq, 1)), dk_ref, dv_ref, got_ref, d_ref, rows, width, (give_send, give_recv))
        key_extra(work[0], jnp.where(place.side == 0, length_ref[0], length_ref[1]), place.core, 2 * rows, 0)
        late[2].wait()
        xt_ref[...] = x_ref[...].T
        late[0].wait()
        late[1].wait()

        def weight_part(pair):
            for which in range(3):
                cols = pl.ds(which * width + pair * step, step)
                value = nn(xt_ref[...], d_ref[:, cols]).astype(low)
                grad_ref[:, :, :, pl.ds(pair * width + which * step, step)] = value.reshape(*grad_ref.shape[:3], step)

        before, amid = [], []
        for k in range(slabs):
            before.append(steps[next(clock) - first])
            amid.append(steps[next(clock) - first] if k != slabs - 2 else [])

        def when_slab(j, chosen):
            for k, calls in enumerate(chosen):
                if calls:
                    @pl.when(j == k)
                    def _():
                        for call in calls:
                            call()

        def slab_step(j, carry):
            @pl.when(j >= 2)
            def _():
                give.take(j - 2)

            when_slab(j, [[functools.partial(weight_part, k // 2 - 1)] if k % 2 and k > 2 else [] for k in range(slabs)])
            when_slab(j, before)
            slot = lax.rem(j, 2)
            backward_slab(j, block, ins, work, dk_ref.at[slot], dv_ref.at[slot], d_ref, lambda: when_slab(j, amid))
            give.start(j)
            return carry

        lax.fori_loop(0, slabs, slab_step, 0)
        for j in range(slabs - 2, slabs):
            give.take(j)
        weight_part(slabs // 2 - 1)
        for i, base in ((0, 0), (1, 2 * width)):
            small_ref[i:i + 1, :] = column_sum(d_ref[:, pl.ds(base, width)])
        small.begin()
        tick()
        late[3].wait()

        def input_part(t, carry):
            cols = pl.ds(pl.multiple_of(t * step, step), step)
            rows_ref[:, cols] = (base_ref[:, cols] + nt(d_ref[...], w_ref[cols, :])).astype(low)
            return carry

        lax.fori_loop(0, width // step, input_part, 0)

    pl.run_scoped(
        attend, lows(rows, 3 * width), lows(rows, 2 * width), lows(rows, width), lows(width, rows), lows(width, 3 * width),
        lows(rows, 3 * width), full(2, 2 * rows, 128), full(2, 2 * rows, 128), *backward_work(rows),
    )
    moves[1].start()
    for i, now in enumerate(clock):
        for call in steps[now - first]:
            call()
        if i % 2 and i < 8:
            small.advance(i // 2)
    small.finish()
    share = width // dp_size
    turned = pltpu.roll(small_out[0:8, :], lax.rem(width - place.dp * share, width), 1)
    for i in range(8):
        vec_outs[i][...] = turned[i:i + 1, 0:share]
    wide = small_out[pl.ds(8 + place.z, 1), :]
    vec_outs[8][...] = jnp.where(place.y == 0, wide[:, :width // 2], wide[:, width // 2:])
    for move in moves:
        move.wait()


def decode(dp_size, lengths, ins, out_shapes, part_shapes, plan, rows_shape):
    x = ins[4]
    rows, width = x.shape
    z, loads = dp_size // 2, sum(1 for p in plan if p[0] < len(part_shapes))
    slabs, dma = width // 128, pltpu.SemaphoreType.DMA
    anywhere, vmem = pl.BlockSpec(memory_space=pl.ANY), pl.BlockSpec(memory_space=pltpu.VMEM)
    low = lambda *shape: pltpu.VMEM(shape, jnp.bfloat16)
    full = lambda *shape: pltpu.VMEM(shape, jnp.float32)
    sds = lambda shape, dtype: jax.ShapeDtypeStruct(shape, dtype)
    return pl.pallas_call(
        functools.partial(decode_kernel, dp_size, plan, loads, min(512, rows)),
        out_shape=[sds(s, jnp.float32) for s in out_shapes] + [sds((1, width // dp_size), jnp.float32)] * 8
        + [sds((1, width // 2), jnp.float32)] + [sds(rows_shape, jnp.bfloat16)] * 2 + [sds(s, jnp.bfloat16) for s in part_shapes],
        in_specs=[pl.BlockSpec(memory_space=pltpu.SMEM)] + [anywhere] * len(ins),
        out_specs=[anywhere] * 6 + [vmem] * 9 + [anywhere] * (2 + len(part_shapes)),
        scratch_shapes=[
            full(slabs, 2, rows, 128), dma((slabs, 2)), dma((slabs, 2)), low(rows, width), low(rows, width), full(rows, width),
            low(rows, width), full(rows, 128), low(rows, width), full(8, width), full(8, width),
            full(16, width), full(16, width), dma((2, 3)), dma((6,)), dma((4,)), dma((5, 2)), low(z, 2, plan[0][2], 3 * width),
            full(4, 16, width), full(z + 2, 16, width), dma((z + 2,)), dma((z + 2,)),
        ] + reduce_scratch(dp_size, len(plan), loads, plan[0][2], plan[0][4]),
        compiler_params=pltpu.CompilerParams(collective_id=3, has_side_effects=True, vmem_limit_bytes=62 << 20),
        name="decode",
    )(lengths, *ins)


def settle_kernel(count, *refs):
    srcs, dsts, bufs, sem = refs[:count], refs[count:2 * count], refs[2 * count:3 * count], refs[3 * count]
    gets = [pltpu.make_async_copy(a, b, sem.at[0, i]) for i, (a, b) in enumerate(zip(srcs, bufs))]
    puts = [pltpu.make_async_copy(a.at[0] if len(a.shape) > len(b.shape) else a, b, sem.at[1, i])
            for i, (a, b) in enumerate(zip(bufs, dsts))]
    for get in gets:
        get.start()
    for get, put in zip(gets, puts):
        get.wait()
        put.start()
    for put in puts:
        put.wait()


def settle(arrays):
    count = len(arrays)
    anywhere = pl.BlockSpec(memory_space=pl.ANY)
    shape = lambda a: a.shape[1:] if a.shape[0] == 1 else a.shape
    return pl.pallas_call(
        functools.partial(settle_kernel, count),
        out_shape=[jax.ShapeDtypeStruct(shape(a), a.dtype) for a in arrays],
        in_specs=[anywhere] * count,
        out_specs=[anywhere] * count,
        scratch_shapes=[pltpu.VMEM(a.shape, a.dtype) for a in arrays] + [pltpu.SemaphoreType.DMA((2, count))],
        compiler_params=pltpu.CompilerParams(vmem_limit_bytes=61 << 20),
        name="settle",
    )(*arrays)


def matmul(a, b):
    return jnp.dot(a, b, preferred_element_type=jnp.float32)


def inner_rows(a, b):
    return lax.dot_general(a, b, (((0,), (0,)), ((), ())), preferred_element_type=jnp.float32)


def times_transposed(a, b):
    return lax.dot_general(a, b, (((1,), (1,)), ((), ())), preferred_element_type=jnp.float32)


def swap_rows(rows):
    side = lax.div(lax.axis_index("seq"), 2)
    size = lax.axis_size("seq")
    got = lax.ppermute(lax.dynamic_index_in_dim(rows, 1 - side, 0, False), "seq", [(i, i ^ 2) for i in range(size)])
    kept = lax.dynamic_index_in_dim(rows, side, 0, False)
    first = jnp.where(side == 0, kept, got)
    second = jnp.where(side == 0, got, kept)
    return jnp.concatenate([first, second], axis=0)


def swap_rows_back(rows):
    side = lax.div(lax.axis_index("seq"), 2)
    size = lax.axis_size("seq")
    blocks = rows.reshape(2, rows.shape[0] // 2, rows.shape[1])
    got = lax.ppermute(lax.dynamic_index_in_dim(blocks, 1 - side, 0, False), "seq", [(i, i ^ 2) for i in range(size)])
    kept = lax.dynamic_index_in_dim(blocks, side, 0, False)
    return jnp.stack([jnp.where(side == 0, kept, got), jnp.where(side == 0, got, kept)])


def pack_vectors(narrow, wide):
    rows = jnp.stack([v.astype(jnp.float32) for v in narrow])
    rows = jnp.pad(rows, ((0, 0), (0, 128 - rows.shape[1])))
    more = wide.astype(jnp.float32).reshape(-1, 128)
    both = jnp.concatenate([rows, more], axis=0)
    return jnp.pad(both, ((0, 16 - both.shape[0]), (0, 0)))


def norm_stats(hidden):
    row_mean = jnp.mean(hidden, axis=-1, keepdims=True)
    centred = hidden - row_mean
    row_var = jnp.mean(centred * centred, axis=-1, keepdims=True)
    scale = lax.rsqrt(row_var + eps_norm)
    return centred * scale, scale


def norm_backward(grad, gain, unit, scale):
    e = grad * gain
    first = jnp.mean(e, axis=-1, keepdims=True)
    second = jnp.mean(e * unit, axis=-1, keepdims=True)
    return scale * (e - first - unit * second)


def col_sum(value):
    return jnp.sum(value, axis=0)


def local(
    inputs, lengths, query_weight, key_weight, value_weight, output_weight, up_weight, down_weight,
    query_bias, value_bias, output_bias, up_bias, down_bias, first_gain, first_shift, second_gain, second_shift, cotangent,
):
    dp_size = lax.axis_size("dp")
    groups, length, width = inputs.shape
    shard = query_weight.shape[0]
    fast = dp_size == 8 and shard == 96 and groups == 2
    rows = groups * length
    seq = lax.axis_index("seq")
    core, side = lax.rem(seq, 2), lax.div(seq, 2)
    narrow = [query_bias, value_bias, output_bias, down_bias, first_gain, first_shift, second_gain, second_shift]
    hidden_width = up_weight.shape[1]
    if fast:
        u = shard
        half = width // 2
        cuts = [(i, 0, 0, 0, width * i) for i in (1, 2, 0)] + [(3, 1, 0, 0, 0)]
        cuts += [(4, 2, 0, width * j, width * j) for j in range(hidden_width // width)]
        plan = [(s, d, row, u, col + half * h, half, to + half * h) for s, d, row, col, to in cuts for h in range(2)]
        plan += [(5, 3, u * j, u, half * h, half, half * h) for h in range(2) for j in range(down_weight.shape[0] // u)]
        plan = [(*p, i < len(plan) - 6) for i, p in enumerate(plan)]
        weights = [query_weight, key_weight, value_weight, output_weight, up_weight, down_weight]
        shapes = [(u, 3 * width), (u, width), (u, hidden_width), (down_weight.shape[0], width)]
        (qkv_w, out_w, up_w, down_w, flat_in, qkv, context, lse, other, first_norm, unit_1, scale_1, hidden_act, slope,
         second_sum_grad, layer_rows, sums, flat_vec) = encode(
            dp_size, lengths, weights, shapes, plan, pack_vectors(narrow, up_bias), inputs, cotangent
        )
        qkv_w, out_w = qkv_w.reshape(width, 3 * width), out_w.reshape(width, width)
        up_w, down_w = up_w.reshape(width, hidden_width), down_w.reshape(hidden_width, width)
    else:
        gather = lambda a: lax.all_gather(a, "dp", axis=0, tiled=True)
        qkv_w = gather(jnp.concatenate([query_weight, key_weight, value_weight], axis=1))
        out_w, up_w, down_w = gather(output_weight), gather(up_weight), gather(down_weight)
        flat_vec = jnp.stack([gather(v.astype(jnp.float32)) for v in narrow])
        bias_up = gather(up_bias.astype(jnp.float32))
        flat_in, flat_cot = swap_rows(inputs), swap_rows(cotangent)
    bias_q, bias_v, bias_out, bias_down, gain_1, shift_1, gain_2, shift_2 = [flat_vec[i] for i in range(8)]
    if not fast:
        bias_qkv = jnp.concatenate([bias_q, jnp.zeros_like(bias_q), bias_v])
        qkv = (matmul(flat_in, qkv_w) + bias_qkv).astype(jnp.bfloat16)
        context, lse, other = attend_forward(lengths, qkv)
        first_sum = flat_in.astype(jnp.float32) + (matmul(context, out_w) + bias_out)
        unit_1, scale_1 = norm_stats(first_sum)
        first_norm = (unit_1 * gain_1 + shift_1).astype(jnp.bfloat16)
        up_pre = matmul(first_norm, up_w) + bias_up
        below = 0.5 + 0.5 * lax.erf(up_pre * (0.5 ** 0.5))
        hidden_act = (up_pre * below).astype(jnp.bfloat16)
        slope = (below + up_pre * jnp.exp(-0.5 * up_pre * up_pre) * 0.3989422804014327).astype(jnp.bfloat16)
        down_out = matmul(hidden_act, down_w) + bias_down
        second_sum = first_norm.astype(jnp.float32) + down_out
        unit_2, scale_2 = norm_stats(second_sum)
        layer_rows = (unit_2 * gain_2 + shift_2).astype(jnp.bfloat16)

        row = jnp.arange(rows)
        position = lax.rem(row, length) + (core + 2 * lax.div(row, length)) * length
        live = (position < lengths[side]).astype(jnp.float32)
        grad_out = flat_cot.astype(jnp.float32) * live[:, None]
        second_gain_grad, second_shift_grad = col_sum(grad_out * unit_2), col_sum(grad_out)
        second_sum_grad = norm_backward(grad_out, gain_2, unit_2, scale_2)
        down_bias_grad = col_sum(second_sum_grad.astype(jnp.bfloat16).astype(jnp.float32))
    low = jnp.bfloat16
    if not fast:
        down_low = second_sum_grad.astype(jnp.bfloat16)
        down_w_grad = inner_rows(hidden_act, down_low).astype(low)
        up_low = (times_transposed(down_low, down_w) * slope.astype(jnp.float32)).astype(low)
        up_w_grad = inner_rows(first_norm, up_low).astype(low)
        up_bias_grad = col_sum(up_low.astype(jnp.float32))
        norm_grad = second_sum_grad + times_transposed(up_low, up_w)
        first_gain_grad, first_shift_grad = col_sum(norm_grad * unit_1), col_sum(norm_grad)
        first_sum_grad = norm_backward(norm_grad, gain_1, unit_1, scale_1)
        attended_low = first_sum_grad.astype(low)
        out_w_grad = inner_rows(context, attended_low).astype(low)
        out_bias_grad = col_sum(attended_low.astype(jnp.float32))
        context_grad = times_transposed(attended_low, out_w).astype(low)
        qkv_low = attend_backward(lengths, qkv, other, context, context_grad, lse)
        qkv_w_grad = inner_rows(flat_in, qkv_low)
        qkv_bias_grad = col_sum(qkv_low.astype(jnp.float32))
        input_rows = (first_sum_grad + times_transposed(qkv_low, qkv_w)).astype(low)
        small = jnp.concatenate([
            jnp.stack([qkv_bias_grad[:width], qkv_bias_grad[2 * width:], out_bias_grad, down_bias_grad, first_gain_grad,
                       first_shift_grad, second_gain_grad, second_shift_grad]),
            up_bias_grad.reshape(-1, width),
        ], axis=0)
    me = lax.axis_index("dp")
    if fast:
        plan = [(0, u * j, u, half * h, half, u * j, [(0, half, 5, half * h)]) for j in range(down_weight.shape[0] // u) for h in range(2)]
        plan += [(1, 0, u, half * i, half, 0, [(0, half, 4, half * i)]) for i in range(hidden_width // half)]
        plan += [(2, 0, u, half * h, half, 0, [(0, half, 3, half * h)]) for h in range(2)]
        for p in range(width // 256):
            plan.append((3, 0, u, width * p, half, 0, [(0, 256, 0, 256 * p), (256, 128, 1, 256 * p)]))
            plan.append((3, 0, u, width * p + half, half, 0, [(0, 128, 1, 256 * p + 128), (128, 256, 2, 256 * p)]))
        plan = [(*p, 2 <= i < len(plan) - 8) for i, p in enumerate(plan)]
        shapes = [(u, width)] * 4 + [up_weight.shape, down_weight.shape]
        halves_of = lambda shape: (dp_size // 2, 2, *shape)
        part_shapes = [halves_of(down_weight.shape), halves_of(up_weight.shape), halves_of(output_weight.shape)]
        ins = (qkv, other, context, lse, flat_in, qkv_w, out_w, up_w, down_w, first_norm, unit_1, scale_1, hidden_act, slope,
               second_sum_grad, layer_rows, sums, flat_vec)
        results = decode(dp_size, lengths, ins, shapes, part_shapes, plan, (groups, length, width))
        mine, layer_out, input_grad = results[:15], results[15], results[16]
        layer_out, input_grad, *mine = settle((layer_out, input_grad, *mine))
        weight_grads, mine = mine[:6], mine[6:]
        up_mine = mine.pop()
    else:
        scatter = lambda a: lax.psum(lax.psum_scatter(a.astype(jnp.float32), "dp", scatter_dimension=0, tiled=True), "seq")
        qkv_g = scatter(qkv_w_grad)
        weight_grads = [qkv_g[:, :width], qkv_g[:, width:2 * width], qkv_g[:, 2 * width:]]
        weight_grads += [scatter(out_w_grad), scatter(up_w_grad), scatter(down_w_grad)]
        small = lax.psum(small, ("dp", "seq"))
        layer_out, input_grad = swap_rows_back(layer_rows), swap_rows_back(input_rows)
        part = query_bias.shape[0]
        mine = list(lax.dynamic_slice(small, (0, me * part), (8, part)))
        up_part = up_bias.shape[0]
        up_mine = lax.dynamic_slice(small[8:8 + hidden_width // width].reshape(hidden_width), (me * up_part,), (up_part,))
    return (layer_out, input_grad, *weight_grads, mine[0], mine[1], mine[2], up_mine, *mine[3:8])


def solution(mesh):
    rows, matrix, vector = P("dp", "seq", None), P("dp", None), P("dp")
    return jax.shard_map(
        local,
        mesh=mesh,
        in_specs=(rows, vector, *[matrix] * 6, *[vector] * 9, rows),
        out_specs=(rows, rows, *[matrix] * 6, *[vector] * 9),
        check_vma=False,
    )
```

profile of v0, /device:TPU:0, one launch (start us, length us, event | category | flops | bytes accessed | tf_op | source)
XLA Modules:
  0.0 213.8 jit_solution(15677734249420398409)
XLA Ops:
  0.7 0.8 stack.44
  1.5 0.7 fusion.1
  2.1 0.6 pad_convert_fusion.refs_6_
  2.7 94.7 %encode.1 = (bf16[4,2,96,2304]{3,2,1,0:T(8,128)(2,1)}, bf16[4,2,96,768]{3,2,1,0:T(8,128)(2,1)}, bf16[4,2,96,3072]{3,2,1,0:T(8,128)(2,1)}, bf16[4,2,384,768]{3,2,...) custom-call(s32[2]{0:T(128)} %length_ref.3, ...), custom_call_target="tpu_custom_call" | custom-call | tf_op jit(solution)/shard_map/encode/pallas_call | solution.py:961
  97.5 111.4 %decode.1 = (f32[96,768]{1,0:T(8,128)}, f32[96,768]{1,0:T(8,128)}, f32[96,768]{1,0:T(8,128)}, f32[96,768]{1,0:T(8,128)}, f32[96,3072]{1,0:T(8,128)}, /*index=5*/...) custom-call(s32[2]{0:T(128)} %length_ref.3, ...), custom_call_target="tpu_custom_call" | custom-call | tf_op jit(solution)/shard_map/decode/pallas_call | solution.py:1240
  208.9 4.8 %settle.1 = (bf16[2,256,768]{2,1,0:T(8,128)(2,1)}, bf16[2,256,768]{2,1,0:T(8,128)(2,1)}, f32[96,768]{1,0:T(8,128)}, f32[96,768]{1,0:T(8,128)}, f32[96,768]{1,0:T...) custom-call(bf16[2,256,768]{2,1,0:T(8,128)(2,1)} %get-tuple-element., ...), custom_call_target="tpu_custom_call" | custom-call | tf_op jit(solution)/shard_map/settle/pallas_call | solution.py:1275
where the time goes:
time: 214 us
  Pallas kernels  211 us (99%)
    pallas_call x1, Pallas kernels, decode(): pl.pallas_call(functools.partial(decode_kernel, dp_size, plan, loads, min...  111 us
    pallas_call x1, Pallas kernels, encode(): pl.pallas_call(functools.partial(encode_kernel, dp_size, plan, window, mi...  94.7 us
    pallas_call x1, Pallas kernels, settle(): pl.pallas_call(functools.partial(settle_kernel, count), out_shape=[jax.Sh...  4.77 us

commit v1 on v0

--- a/solution.py
+++ b/solution.py
@@ -1361,7 +1361,7 @@
         cuts += [(4, 2, 0, width * j, width * j) for j in range(hidden_width // width)]
         plan = [(s, d, row, u, col + half * h, half, to + half * h) for s, d, row, col, to in cuts for h in range(2)]
         plan += [(5, 3, u * j, u, half * h, half, half * h) for h in range(2) for j in range(down_weight.shape[0] // u)]
-        plan = [(*p, i < len(plan) - 6) for i, p in enumerate(plan)]
+        plan = [(*p, i < len(plan) - 9) for i, p in enumerate(plan)]
         weights = [query_weight, key_weight, value_weight, output_weight, up_weight, down_weight]
         shapes = [(u, 3 * width), (u, width), (u, hidden_width), (down_weight.shape[0], width)]
         (qkv_w, out_w, up_w, down_w, flat_in, qkv, context, lse, other, first_norm, unit_1, scale_1, hidden_act, slope,
@@ -1432,7 +1432,7 @@
         for p in range(width // 256):
             plan.append((3, 0, u, width * p, half, 0, [(0, 256, 0, 256 * p), (256, 128, 1, 256 * p)]))
             plan.append((3, 0, u, width * p + half, half, 0, [(0, 128, 1, 256 * p + 128), (128, 256, 2, 256 * p)]))
-        plan = [(*p, 2 <= i < len(plan) - 8) for i, p in enumerate(plan)]
+        plan = [(*p, 1 <= i < len(plan) - 5) for i, p in enumerate(plan)]
         shapes = [(u, width)] * 4 + [up_weight.shape, down_weight.shape]
         halves_of = lambda shape: (dp_size // 2, 2, *shape)
         part_shapes = [halves_of(down_weight.shape), halves_of(up_weight.shape), halves_of(output_weight.shape)]

time: 214 us -> 206 us (0.963)
  Pallas kernels: 211 us -> 203 us
    pallas_call x1, Pallas kernels: 111 us -> 103 us  [decode(): pl.pallas_call(functools.partial(decode_kernel, dp_size, plan, loads, min...]
where the time goes in v1:
time: 206 us
  Pallas kernels  203 us (99%)
    pallas_call x1, Pallas kernels, decode(): pl.pallas_call(functools.partial(decode_kernel, dp_size, plan, loads, min...  103 us
    pallas_call x1, Pallas kernels, encode(): pl.pallas_call(functools.partial(encode_kernel, dp_size, plan, window, mi...  95 us
    pallas_call x1, Pallas kernels, settle(): pl.pallas_call(functools.partial(settle_kernel, count), out_shape=[jax.Sh...  4.77 us

profile of v1, /device:TPU:0, one launch (start us, length us, event | category | flops | bytes accessed | tf_op | source)
XLA Modules:
  0.0 206.0 jit_solution(14666781310403541278)
XLA Ops:
  0.7 0.8 stack.44
  1.5 0.7 fusion.1
  2.1 0.6 pad_convert_fusion.refs_6_
  2.7 95.0 %encode.1 = (bf16[4,2,96,2304]{3,2,1,0:T(8,128)(2,1)}, bf16[4,2,96,768]{3,2,1,0:T(8,128)(2,1)}, bf16[4,2,96,3072]{3,2,1,0:T(8,128)(2,1)}, bf16[4,2,384,768]{3,2,...) custom-call(s32[2]{0:T(128)} %length_ref.3, ...), custom_call_target="tpu_custom_call" | custom-call | tf_op jit(solution)/shard_map/encode/pallas_call | solution.py:961
  97.8 103.3 %decode.1 = (f32[96,768]{1,0:T(8,128)}, f32[96,768]{1,0:T(8,128)}, f32[96,768]{1,0:T(8,128)}, f32[96,768]{1,0:T(8,128)}, f32[96,3072]{1,0:T(8,128)}, /*index=5*/...) custom-call(s32[2]{0:T(128)} %length_ref.3, ...), custom_call_target="tpu_custom_call" | custom-call | tf_op jit(solution)/shard_map/decode/pallas_call | solution.py:1240
  201.1 4.8 %settle.1 = (bf16[2,256,768]{2,1,0:T(8,128)(2,1)}, bf16[2,256,768]{2,1,0:T(8,128)(2,1)}, f32[96,768]{1,0:T(8,128)}, f32[96,768]{1,0:T(8,128)}, f32[96,768]{1,0:T...) custom-call(bf16[2,256,768]{2,1,0:T(8,128)(2,1)} %get-tuple-element., ...), custom_call_target="tpu_custom_call" | custom-call | tf_op jit(solution)/shard_map/settle/pallas_call | solution.py:1275
